TPU v7x, 512 devices: a whole 4x8x8 slice. The times are simulated.
512 devices in a mesh: gx: 16 (over y, core), gy: 8 (over z), gz: 4 (over x).
Axes of the slice: x: 4, y: 8, z: 8, core: 2. Of those that a mesh axis runs over, the one named last changes fastest.
Arguments:
- noise: float32 [32, 64, 64, 512], P(None, 'gx', 'gy', 'gz'), may hold values from -32 to 32
- basis: float32 [192, 64, 64, 512], P(None, 'gx', 'gy', 'gz'), may hold values from -5 to 5
- conductivity: float32 [64, 64, 512], P('gx', 'gy', 'gz'), may hold values from 0.2 to 2
- reaction: float32 [64, 64, 512], P('gx', 'gy', 'gz'), may hold values from 0.05 to 0.5
Outputs:
- new_block: float32 [32, 64, 64, 512], P(None, 'gx', 'gy', 'gz')
- factor: float32 [32, 32], replicated
- projection: float32 [192, 32], replicated
All inputs are finite; a program needn't handle non-finite values.
Results may differ from a plain program's by a relative error of at most 0.00012.
Values sent between devices are 32-bit elements; how exact they have to be, the bound alone decides.
No kernel may reach another device: no remote copies, remote signals or barrier semaphores. Data moves between devices by JAX's collectives and lax.ppermute only.
A program may use at most 64 MiB of HBM per device.

v0:
```python
import jax
import jax.numpy as jnp
from jax import lax
from jax.sharding import PartitionSpec as P


def padded(value, sides, width):
    for axis, dim in sides:
        size, length = (lax.axis_size(axis), value.shape[dim])
        up = [(i, (i + 1) % size) for i in range(size - 1)]
        down = [(j, i) for i, j in up]
        last = lax.slice_in_dim(value, length - width, length, axis=dim)
        initial = lax.slice_in_dim(value, 0, width, axis=dim)
        before = lax.ppermute(last, axis, up)
        after = lax.ppermute(initial, axis, down)
        value = jnp.concatenate([before, value, after], axis=dim)
    return value


def stencil(field_pad, theta_pad, reaction_core):
    theta_core = theta_pad[1:-1, 1:-1, 1:-1]
    value_core = field_pad[:, 1:-1, 1:-1, 1:-1]
    result = reaction_core * value_core
    diagonal = reaction_core
    offsets = (
        (slice(2, None), slice(1, -1), slice(1, -1)),
        (slice(None, -2), slice(1, -1), slice(1, -1)),
        (slice(1, -1), slice(2, None), slice(1, -1)),
        (slice(1, -1), slice(None, -2), slice(1, -1)),
        (slice(1, -1), slice(1, -1), slice(2, None)),
        (slice(1, -1), slice(1, -1), slice(None, -2)),
    )
    for slicer in offsets:
        face_value = 0.5 * (theta_core + theta_pad[slicer])
        result = result + face_value * (value_core - field_pad[(slice(None),) + slicer])
        diagonal = diagonal + face_value
    return (result, diagonal)


def rim_layer(field):
    return padded(field, (("gx", 1), ("gy", 2), ("gz", 3)), 1)


def shards(noise, basis, conductivity, reaction):
    highest = lax.Precision.HIGHEST
    columns = noise.shape[0]
    span_x, span_y, span_z = (noise.shape[1], noise.shape[2], noise.shape[3])
    cell_total = float(
        span_x * span_y * span_z * lax.axis_size("gx") * lax.axis_size("gy") * lax.axis_size("gz")
    )
    extended = rim_layer(jnp.concatenate([noise, conductivity[None]], axis=0))
    theta_pad = extended[columns]
    first, diagonal = stencil(extended[:columns], theta_pad, reaction)
    image, unused = stencil(rim_layer(first / diagonal), theta_pad, reaction)
    basis_flat = basis.reshape(basis.shape[0], -1)
    image_flat = image.reshape(columns, -1)

    def local_product(left, right):
        return lax.dot_general(left, right, (((1,), (1,)), ((), ())), precision=highest)

    def remove(block, coeff):
        return block - lax.dot_general(
            coeff, basis_flat, (((0,), (0,)), ((), ())), precision=highest
        )

    def project(block):
        return lax.psum(local_product(basis_flat, block), ("gx", "gy", "gz")) / cell_total

    def gram_sum(block):
        return lax.psum(local_product(block, block), ("gx", "gy", "gz")) / cell_total

    coeff_one = project(image_flat)
    image_one = remove(image_flat, coeff_one)
    coeff_two = project(image_one)
    image_two = remove(image_one, coeff_two)
    gram_two = gram_sum(image_two)
    lower_one = jnp.linalg.cholesky(gram_two)
    middle = jax.scipy.linalg.solve_triangular(lower_one, image_two, lower=True)
    lower_two = jnp.linalg.cholesky(gram_sum(middle))
    new_block = jax.scipy.linalg.solve_triangular(lower_two, middle, lower=True)
    factor = jnp.dot(lower_two.T, lower_one.T, precision=highest)
    return (new_block.reshape(noise.shape), factor, coeff_one + coeff_two)


def solution(mesh):
    return jax.shard_map(
        shards,
        mesh=mesh,
        in_specs=(
            P(None, "gx", "gy", "gz"),
            P(None, "gx", "gy", "gz"),
            P("gx", "gy", "gz"),
            P("gx", "gy", "gz"),
        ),
        out_specs=(P(None, "gx", "gy", "gz"), P(), P()),
        check_vma=False,
    )
```

profile of v0, /device:TPU:26, one launch (start us, length us, event | category | flops | bytes accessed | tf_op | source)
XLA Modules:
  0.0 507.7 jit_solution(3330146122280983451)
XLA Ops:
  0.6 1.2 copy_dynamic-update-slice_fusion
  1.8 0.7 copy_dynamic-update-slice_fusion.1
  2.8 1.9 collective-permute-start
  4.7 3.6 collective-permute-start.1
  8.3 0.8 collective-permute-done
  9.1 1.8 collective-permute-done.1
  11.0 4.3 collective-permute-start.2
  15.3 1.3 collective-permute-start.3
  16.6 1.2 collective-permute-done.2
  17.8 4.7 collective-permute-done.3
  22.5 0.7 copy-done.7
  23.2 0.4 pad_maximum_fusion
  23.6 0.4 fusion.92
  24.0 0.6 copy.33
  24.6 2.4 collective-permute-start.5
  27.0 0.6 copy.32
  27.6 3.4 collective-permute-start.4
  31.0 0.8 copy.35
  31.8 1.7 collective-permute-done.4
  33.5 1.5 copy.34
  35.1 0.9 fusion.53
  36.2 5.2 %fusion.36 = f32[32,4,8,128]{3,1,2,0:T(4,128)S(1)} fusion(f32[33,6,10,1]{3,1,2,0:T(8,128)S(1)} %copy.34, f32[33,6,1,128]{3,1,2,0:T(8,128)S(1)} %copy-done.8, f32[33,6,1,128]{3,1,2,0:T(8,128)S(1)} %copy-done.6, f32[33,1,8,128]{3,1,2,0:T(1,128)S(1)} %collective-permute-done.1, f32[33,4,8,128]{3,1,2,0:T(4,128)S(1)} %copy_dynamic-update-slice_fusion.1, ...), kind=kLoop, calls=%fused_computation.56 | loop fusion | flops 4980736 | bytes 2209248 | tf_op jit(solution)/shard_map/div | solution.py:54
  41.6 3.6 collective-permute-start.7
  45.2 2.0 collective-permute-start.6
  47.2 0.7 collective-permute-done.7
  47.9 2.7 collective-permute-done.6
  50.7 4.3 collective-permute-start.9
  55.0 1.3 collective-permute-start.8
  56.3 1.2 collective-permute-done.9
  57.5 5.9 %collective-permute-done.8 = f32[32,6,1,128]{3,1,2,0:T(8,128)S(1)} collective-permute-done((f32[32,6,1,128]{3,1,2,0:T(8,128)S(1)}, f32[32,6,1,128]{3,1,2,0:T(8,128)S(1)}, u32[]{:S(2)}, u32[]{:S(2)}) %collective-permute-start.8) | collective-permute-done | bytes 98336 | tf_op jit(solution)/shard_map/ppermute | solution.py:15
  63.4 0.6 copy-done.9
  64.5 0.4 fusion.93
  64.9 0.5 copy.45
  65.4 1.9 collective-permute-start.10
  67.3 0.5 copy.47
  67.8 4.1 collective-permute-start.11
  71.9 1.6 copy.46
  73.6 1.6 copy.48
  75.2 5.8 %fusion.17 = f32[32,4,8,128]{3,1,2,0:T(4,128)S(1)} fusion(f32[32,4,8,128]{3,1,2,0:T(4,128)} %copy-done.1, f32[32,6,10,1]{3,1,2,0:T(8,128)} %copy.48, f32[32,6,1,128]{3,1,2,0:T(8,128)} %copy-done.9, f32[32,6,1,128]{3,1,2,0:T(8,128)S(1)} %collective-permute-done.9, f32[32,1,8,128]{3,1,2,0:T(1,128)S(1)} %collective-permute-done.6, ...), kind=kLoop, calls=%fused_computation.19 | loop fusion | flops 4849664 | bytes 1637376 | tf_op jit(solution)/shard_map/add | solution.py:35
  81.1 0.8 copy.49
  81.9 4.3 fusion.9
  86.2 100.3 %psum.28 = f32[192,32]{0,1:T(8,128)S(1)} all-reduce(f32[192,32]{0,1:T(8,128)S(1)} %fusion.9), channel_id=1, replica_groups=mesh['gx'=16,'gy'=8,'gz'=4] {'gx','gy','gz'}, use_global_device_ids=true, to_apply=%region_0.0 | all-reduce | flops 6144 | bytes 49152 | tf_op jit(solution)/shard_map/psum | solution.py:67
  186.6 4.8 convolution_subtract_fusion.1
  191.4 0.8 copy-done.3
  192.2 4.0 fusion.12
  196.3 96.0 %psum.29 = f32[192,32]{0,1:T(8,128)S(1)} all-reduce(f32[192,32]{0,1:T(8,128)S(1)} %fusion.12), channel_id=1, replica_groups=mesh['gx'=16,'gy'=8,'gz'=4] {'gx','gy','gz'}, use_global_device_ids=true, to_apply=%region_1.0 | all-reduce | flops 6144 | bytes 49152 | tf_op jit(solution)/shard_map/psum | solution.py:67
  292.3 4.7 convolution_subtract_fusion
  297.0 0.7 multiply_add_fusion
  297.8 0.6 fusion.96
  298.4 94.5 %psum.30 = f32[32,32]{0,1:T(8,128)S(1)} all-reduce(f32[32,32]{0,1:T(8,128)S(1)} %fusion.96), channel_id=1, replica_groups=mesh['gx'=16,'gy'=8,'gz'=4] {'gx','gy','gz'}, use_global_device_ids=true, to_apply=%region_2.0 | all-reduce | flops 1024 | bytes 8192 | tf_op jit(solution)/shard_map/psum | solution.py:70
  393.0 2.9 cholesky.44
  395.9 0.7 compare_reduce_fusion.1
  396.6 0.6 fusion.70
  397.2 2.4 custom-call.6
  399.7 1.7 fusion.64
  401.4 0.6 fusion.97
  401.9 95.4 %psum.31 = f32[32,32]{0,1:T(8,128)S(1)} all-reduce(f32[32,32]{0,1:T(8,128)S(1)} %fusion.97), channel_id=1, replica_groups=mesh['gx'=16,'gy'=8,'gz'=4] {'gx','gy','gz'}, use_global_device_ids=true, to_apply=%region_5.8 | all-reduce | flops 1024 | bytes 8192 | tf_op jit(solution)/shard_map/psum | solution.py:70
  497.4 2.9 cholesky.55
  500.4 0.6 compare_reduce_fusion
  501.0 2.1 fusion.75
  503.1 0.7 select_bitcast_fusion
  503.8 2.4 custom-call.7
  506.2 0.7 convolution_bitcast_fusion
  506.9 0.9 copy.61
  (48 shorter events, 1.6 us)
Async XLA Ops:
  2.8 6.3 %collective-permute-start = (f32[33,1,8,128]{3,1,2,0:T(1,128)S(1)}, f32[33,1,8,128]{3,1,2,0:T(1,128)S(1)}, u32[]{:S(2)}, u32[]{:S(2)}) collective-permute-start(f32[33,1,8,128]{3,1,2,0:T(1,128)S(1)} %get-tuple-element.20), channel_id=1, source_target_pairs={{0,32},{32,64},{64,96},{96,128},{128,160},{160,192},{192,224},{224... | collective-permute-start | bytes 405512 | tf_op jit(solution)/shard_map/ppermute | solution.py:14
  4.7 6.2 %collective-permute-start.1 = (f32[33,1,8,128]{3,1,2,0:T(1,128)S(1)}, f32[33,1,8,128]{3,1,2,0:T(1,128)S(1)}, u32[]{:S(2)}, u32[]{:S(2)}) collective-permute-start(f32[33,1,8,128]{3,1,2,0:T(1,128)S(1)} %get-tuple-element.21), channel_id=1, source_target_pairs={{32,0},{64,32},{96,64},{128,96},{160,128},{192,160},{224,192},{256... | collective-permute-start | bytes 405512 | tf_op jit(solution)/shard_map/ppermute | solution.py:15
  11.0 6.8 %collective-permute-start.2 = (f32[33,6,1,128]{3,1,2,0:T(8,128)S(1)}, f32[33,6,1,128]{3,1,2,0:T(8,128)S(1)}, u32[]{:S(2)}, u32[]{:S(2)}) collective-permute-start(f32[33,6,1,128]{3,1,2,0:T(8,128)S(1)} %get-tuple-element.16), channel_id=1, source_target_pairs={{0,4},{4,8},{8,12},{12,16},{16,20},{20,24},{24,28},{1,5},{5,9},{9,... | collective-permute-start | bytes 304136 | tf_op jit(solution)/shard_map/ppermute | solution.py:14
  15.3 7.3 %collective-permute-start.3 = (f32[33,6,1,128]{3,1,2,0:T(8,128)S(1)}, f32[33,6,1,128]{3,1,2,0:T(8,128)S(1)}, u32[]{:S(2)}, u32[]{:S(2)}) collective-permute-start(f32[33,6,1,128]{3,1,2,0:T(8,128)S(1)} %get-tuple-element.17), channel_id=1, source_target_pairs={{4,0},{8,4},{12,8},{16,12},{20,16},{24,20},{28,24},{5,1},{9,5},{13... | collective-permute-start | bytes 304136 | tf_op jit(solution)/shard_map/ppermute | solution.py:15
  17.8 4.7 copy-start.5
  22.5 0.7 copy-start.7
  24.6 6.4 %collective-permute-start.5 = (f32[33,6,10,1]{0,3,2,1:T(1,128)S(1)}, f32[33,6,10,1]{0,3,2,1:T(1,128)S(1)}, u32[]{:S(2)}, u32[]{:S(2)}) collective-permute-start(f32[33,6,10,1]{0,3,2,1:T(1,128)S(1)} %copy.33), channel_id=1, source_target_pairs={{1,0},{2,1},{3,2},{5,4},{6,5},{7,6},{9,8},{10,9},{11,10},{13,12},{... | collective-permute-start | bytes 23768 | tf_op jit(solution)/shard_map/ppermute | solution.py:15
  27.6 5.9 %collective-permute-start.4 = (f32[33,6,10,1]{0,3,2,1:T(1,128)S(1)}, f32[33,6,10,1]{0,3,2,1:T(1,128)}, u32[]{:S(2)}, u32[]{:S(2)}) collective-permute-start(f32[33,6,10,1]{0,3,2,1:T(1,128)S(1)} %copy.32), channel_id=1, source_target_pairs={{0,1},{1,2},{2,3},{4,5},{5,6},{6,7},{8,9},{9,10},{10,11},{12,13},{... | collective-permute-start | bytes 23768 | tf_op jit(solution)/shard_map/ppermute | solution.py:14
  35.0 1.0 copy-start.16
  35.0 1.1 copy-start.4
  35.0 1.1 copy-start.6
  35.0 1.1 copy-start.8
  36.1 5.3 %copy-start.10 = (f32[4,8,128]{2,0,1:T(4,128)}, f32[4,8,128]{2,0,1:T(4,128)S(1)}, u32[]{:S(2)}) copy-start(f32[4,8,128]{2,0,1:T(4,128)S(1)} %get-tuple-element.7) | copy-start | bytes 49156
  36.1 5.3 %copy-start.11 = (f32[4,8,128]{2,0,1:T(4,128)}, f32[4,8,128]{2,0,1:T(4,128)S(1)}, u32[]{:S(2)}) copy-start(f32[4,8,128]{2,0,1:T(4,128)S(1)} %get-tuple-element.8) | copy-start | bytes 49156
  36.1 5.3 %copy-start.12 = (f32[4,8,128]{2,0,1:T(4,128)}, f32[4,8,128]{2,0,1:T(4,128)S(1)}, u32[]{:S(2)}) copy-start(f32[4,8,128]{2,0,1:T(4,128)S(1)} %get-tuple-element.9) | copy-start | bytes 49156
  36.1 5.3 %copy-start.13 = (f32[4,8,128]{2,0,1:T(4,128)}, f32[4,8,128]{2,0,1:T(4,128)S(1)}, u32[]{:S(2)}) copy-start(f32[4,8,128]{2,0,1:T(4,128)S(1)} %get-tuple-element.10) | copy-start | bytes 49156
  36.1 5.3 %copy-start.14 = (f32[4,8,128]{2,0,1:T(4,128)}, f32[4,8,128]{2,0,1:T(4,128)S(1)}, u32[]{:S(2)}) copy-start(f32[4,8,128]{2,0,1:T(4,128)S(1)} %get-tuple-element.11) | copy-start | bytes 49156
  36.2 5.3 %copy-start.15 = (f32[4,8,128]{2,0,1:T(4,128)}, f32[4,8,128]{2,0,1:T(4,128)S(1)}, u32[]{:S(2)}) copy-start(f32[4,8,128]{2,0,1:T(4,128)S(1)} %get-tuple-element.24) | copy-start | bytes 49156
  41.4 22.0 %copy-start.1 = (f32[32,4,8,128]{3,1,2,0:T(4,128)}, f32[32,4,8,128]{3,1,2,0:T(4,128)S(1)}, u32[]{:S(2)}) copy-start(f32[32,4,8,128]{3,1,2,0:T(4,128)S(1)} %fusion.36) | copy-start | bytes 1572868
  41.6 6.3 %collective-permute-start.7 = (f32[32,1,8,128]{3,1,2,0:T(1,128)S(1)}, f32[32,1,8,128]{3,1,2,0:T(1,128)S(1)}, u32[]{:S(2)}, u32[]{:S(2)}) collective-permute-start(f32[32,1,8,128]{3,1,2,0:T(1,128)S(1)} %get-tuple-element.22), channel_id=1, source_target_pairs={{0,32},{32,64},{64,96},{96,128},{128,160},{160,192},{192,224},{224... | collective-permute-start | bytes 393224 | tf_op jit(solution)/shard_map/ppermute | solution.py:14
  45.2 5.4 %collective-permute-start.6 = (f32[32,1,8,128]{3,1,2,0:T(1,128)S(1)}, f32[32,1,8,128]{3,1,2,0:T(1,128)S(1)}, u32[]{:S(2)}, u32[]{:S(2)}) collective-permute-start(f32[32,1,8,128]{3,1,2,0:T(1,128)S(1)} %get-tuple-element.23), channel_id=1, source_target_pairs={{32,0},{64,32},{96,64},{128,96},{160,128},{192,160},{224,192},{256... | collective-permute-start | bytes 393224 | tf_op jit(solution)/shard_map/ppermute | solution.py:15
  50.7 6.8 %collective-permute-start.9 = (f32[32,6,1,128]{3,1,2,0:T(8,128)S(1)}, f32[32,6,1,128]{3,1,2,0:T(8,128)S(1)}, u32[]{:S(2)}, u32[]{:S(2)}) collective-permute-start(f32[32,6,1,128]{3,1,2,0:T(8,128)S(1)} %get-tuple-element.18), channel_id=1, source_target_pairs={{0,4},{4,8},{8,12},{12,16},{16,20},{20,24},{24,28},{1,5},{5,9},{9,... | collective-permute-start | bytes 294920 | tf_op jit(solution)/shard_map/ppermute | solution.py:14
  55.0 8.4 %collective-permute-start.8 = (f32[32,6,1,128]{3,1,2,0:T(8,128)S(1)}, f32[32,6,1,128]{3,1,2,0:T(8,128)S(1)}, u32[]{:S(2)}, u32[]{:S(2)}) collective-permute-start(f32[32,6,1,128]{3,1,2,0:T(8,128)S(1)} %get-tuple-element.19), channel_id=1, source_target_pairs={{4,0},{8,4},{12,8},{16,12},{20,16},{24,20},{28,24},{5,1},{9,5},{13... | collective-permute-start | bytes 294920 | tf_op jit(solution)/shard_map/ppermute | solution.py:15
  63.4 0.6 copy-start.9
  65.4 6.5 %collective-permute-start.10 = (f32[32,6,10,1]{0,3,2,1:T(1,128)S(1)}, f32[32,6,10,1]{0,3,2,1:T(1,128)S(1)}, u32[]{:S(2)}, u32[]{:S(2)}) collective-permute-start(f32[32,6,10,1]{0,3,2,1:T(1,128)S(1)} %copy.45), channel_id=1, source_target_pairs={{1,0},{2,1},{3,2},{5,4},{6,5},{7,6},{9,8},{10,9},{11,10},{13,12},{... | collective-permute-start | bytes 23048 | tf_op jit(solution)/shard_map/ppermute | solution.py:15
  67.8 5.8 %collective-permute-start.11 = (f32[32,6,10,1]{0,3,2,1:T(1,128)S(1)}, f32[32,6,10,1]{0,3,2,1:T(1,128)S(1)}, u32[]{:S(2)}, u32[]{:S(2)}) collective-permute-start(f32[32,6,10,1]{0,3,2,1:T(1,128)S(1)} %copy.47), channel_id=1, source_target_pairs={{0,1},{1,2},{2,3},{4,5},{5,6},{6,7},{8,9},{9,10},{10,11},{12,13},{... | collective-permute-start | bytes 23048 | tf_op jit(solution)/shard_map/ppermute | solution.py:14
  75.2 6.7 %copy-start = (f32[192,4,8,128]{3,2,1,0:T(8,128)S(1)}, f32[192,4,8,128]{3,2,1,0:T(8,128)}, u32[]{:S(2)}) copy-start(f32[192,4,8,128]{3,2,1,0:T(8,128)} %param.8) | copy-start | bytes 9437188
  191.4 0.8 copy-start.3
  297.0 0.8 copy-start.2
where the time goes:
time: 509 us; the launch traced here: 508 us
  blocking collectives  386 us (76%)
  starting transfers between devices  34.1 us (7%)
  other arithmetic  27 us (5%)
  matrix products  23.4 us (5%)
  waiting for transfers between devices  20.8 us (4%)
  local copies, waits for them, and re-layouts  15 us (3%)
    psum x2, blocking collectives, project(): lax.psum(local_product(basis_flat, block), ('gx', 'gy', 'gz')) / cell_total  196 us
    psum x2, blocking collectives, gram_sum(): lax.psum(local_product(block, block), ('gx', 'gy', 'gz')) / cell_total  190 us
    ppermute x6, starting transfers between devices, padded(): before = lax.ppermute(last, axis, up)  21.5 us
    ppermute x6, waiting for transfers between devices, padded(): after = lax.ppermute(initial, axis, down)  15.1 us
    ppermute x6, starting transfers between devices, padded(): after = lax.ppermute(initial, axis, down)  12.6 us
  transfers between devices with their start and end apart: 12, of which 9 were waited for; matrix products, arithmetic and copies ran while one was open for 1% of the time, Pallas kernels for 0%

commit v1 on v0

--- a/solution.py
+++ b/solution.py
@@ -67,7 +67,7 @@
         return lax.psum(local_product(basis_flat, block), ("gx", "gy", "gz")) / cell_total
 
     def gram_sum(block):
-        return lax.psum(local_product(block, block), ("gx", "gy", "gz")) / cell_total
+        return lax.psum(lax.psum(local_product(block, block), ("gy", "gz")), "gx") / cell_total
 
     coeff_one = project(image_flat)
     image_one = remove(image_flat, coeff_one)

time: 509 us -> 687 us (1.35)
  the two profiles are of different devices: /device:TPU:26 before, /device:TPU:32 now
where the time goes in v1:
time: 687 us; the launch traced here: 686 us
  blocking collectives  563 us (82%)
  starting transfers between devices  37.5 us (5%)
  other arithmetic  27.1 us (4%)
  matrix products  23.5 us (3%)
  waiting for transfers between devices  18.7 us (3%)
  local copies, waits for them, and re-layouts  15.1 us (2%)
    psum x2, blocking collectives, gram_sum(): lax.psum(local_product(block, block), ('gy', 'gz'))  278 us
    psum x2, blocking collectives, project(): lax.psum(local_product(basis_flat, block), ('gx', 'gy', 'gz')) / cell_total  193 us
    psum x2, blocking collectives, gram_sum(): lax.psum(lax.psum(local_product(block, block), ('gy', 'gz')), 'gx')  91.5 us
    ppermute x6, starting transfers between devices, padded(): before = lax.ppermute(last, axis, up)  22.7 us
    ppermute x6, starting transfers between devices, padded(): after = lax.ppermute(initial, axis, down)  14.9 us
    ppermute x6, waiting for transfers between devices, padded(): after = lax.ppermute(initial, axis, down)  14.3 us
  transfers between devices with their start and end apart: 12, of which 9 were waited for; matrix products, arithmetic and copies ran while one was open for 1% of the time, Pallas kernels for 0%

profile of v1, /device:TPU:32, one launch (start us, length us, event | category | flops | bytes accessed | tf_op | source)
XLA Modules:
  0.0 686.2 jit_solution(9755889342452332826)
XLA Ops:
  0.6 1.2 copy_dynamic-update-slice_fusion
  1.8 0.7 copy_dynamic-update-slice_fusion.1
  2.8 1.9 collective-permute-start
  4.7 4.9 collective-permute-start.1
  9.6 0.8 collective-permute-done
  10.3 1.8 collective-permute-done.1
  12.2 4.3 collective-permute-start.2
  16.5 1.3 collective-permute-start.3
  17.8 1.4 collective-permute-done.2
  19.2 4.8 collective-permute-done.3
  23.9 0.7 copy-done.7
  25.0 0.4 fusion.92
  25.4 0.6 copy.33
  26.0 1.3 collective-permute-start.5
  27.3 0.6 copy.32
  27.9 5.1 collective-permute-start.4
  33.0 0.8 copy.35
  34.0 1.5 copy.34
  35.5 0.9 fusion.53
  36.7 5.2 fusion.36
  42.1 1.9 collective-permute-start.7
  44.0 4.9 collective-permute-start.6
  48.9 0.7 collective-permute-done.7
  49.6 1.8 collective-permute-done.6
  51.5 4.3 collective-permute-start.9
  55.8 1.3 collective-permute-start.8
  57.1 1.3 collective-permute-done.9
  58.4 6.0 collective-permute-done.8
  64.4 0.7 copy-done.9
  65.4 0.4 fusion.93
  65.8 0.5 copy.45
  66.3 1.3 collective-permute-start.10
  67.6 0.5 copy.47
  68.2 5.1 collective-permute-start.11
  73.3 1.6 copy.46
  74.9 1.6 copy.48
  76.6 5.8 fusion.17
  82.4 0.8 copy.49
  83.2 4.3 fusion.9
  87.6 98.6 %psum.42 = f32[192,32]{0,1:T(8,128)S(1)} all-reduce(f32[192,32]{0,1:T(8,128)S(1)} %fusion.9), channel_id=1, replica_groups=mesh['gx'=16,'gy'=8,'gz'=4] {'gx','gy','gz'}, use_global_device_ids=true, to_apply=%region_0.0 | all-reduce | flops 6144 | bytes 49152 | tf_op jit(solution)/shard_map/psum | solution.py:67
  186.1 4.8 convolution_subtract_fusion.1
  191.0 0.8 copy-done.3
  191.8 4.0 fusion.12
  195.8 94.7 %psum.43 = f32[192,32]{0,1:T(8,128)S(1)} all-reduce(f32[192,32]{0,1:T(8,128)S(1)} %fusion.12), channel_id=1, replica_groups=mesh['gx'=16,'gy'=8,'gz'=4] {'gx','gy','gz'}, use_global_device_ids=true, to_apply=%region_1.0 | all-reduce | flops 6144 | bytes 49152 | tf_op jit(solution)/shard_map/psum | solution.py:67
  290.5 4.7 convolution_subtract_fusion
  295.3 0.7 multiply_add_fusion
  296.1 0.6 fusion.96
  296.6 140.8 %psum.44 = f32[32,32]{0,1:T(8,128)S(1)} all-reduce(f32[32,32]{0,1:T(8,128)S(1)} %fusion.96), channel_id=1, replica_groups=mesh['gx'=16,'gy'=8,'gz'=4] {'gy','gz'}, use_global_device_ids=true, to_apply=%region_2.0 | all-reduce | flops 1024 | bytes 8192 | tf_op jit(solution)/shard_map/psum | solution.py:70
  437.4 45.7 %psum.45 = f32[32,32]{0,1:T(8,128)S(1)} all-reduce(f32[32,32]{0,1:T(8,128)S(1)} %psum.44), channel_id=1, replica_groups=mesh['gx'=16,'gy'=8,'gz'=4] {'gx'}, use_global_device_ids=true, to_apply=%region_3.0 | all-reduce | flops 1024 | bytes 8192 | tf_op jit(solution)/shard_map/psum | solution.py:70
  483.3 2.9 cholesky.44
  486.2 0.7 compare_reduce_fusion.1
  486.9 0.7 fusion.70
  487.6 2.4 custom-call.6
  490.1 1.7 fusion.64
  491.8 0.6 fusion.97
  492.3 137.7 %psum.46 = f32[32,32]{0,1:T(8,128)S(1)} all-reduce(f32[32,32]{0,1:T(8,128)S(1)} %fusion.97), channel_id=1, replica_groups=mesh['gx'=16,'gy'=8,'gz'=4] {'gy','gz'}, use_global_device_ids=true, to_apply=%region_6.9 | all-reduce | flops 1024 | bytes 8192 | tf_op jit(solution)/shard_map/psum | solution.py:70
  630.0 45.7 %psum.47 = f32[32,32]{0,1:T(8,128)S(1)} all-reduce(f32[32,32]{0,1:T(8,128)S(1)} %psum.46), channel_id=1, replica_groups=mesh['gx'=16,'gy'=8,'gz'=4] {'gx'}, use_global_device_ids=true, to_apply=%region_7.10 | all-reduce | flops 1024 | bytes 8192 | tf_op jit(solution)/shard_map/psum | solution.py:70
  675.8 2.9 cholesky.55
  678.8 0.6 compare_reduce_fusion
  679.4 2.2 fusion.75
  681.6 0.7 select_bitcast_fusion
  682.2 2.4 custom-call.7
  684.7 0.7 convolution_bitcast_fusion
  685.3 0.9 copy.61
  (50 shorter events, 2.1 us)
Async XLA Ops:
  2.8 7.5 %collective-permute-start = (f32[33,1,8,128]{3,1,2,0:T(1,128)S(1)}, f32[33,1,8,128]{3,1,2,0:T(1,128)S(1)}, u32[]{:S(2)}, u32[]{:S(2)}) collective-permute-start(f32[33,1,8,128]{3,1,2,0:T(1,128)S(1)} %get-tuple-element.20), channel_id=1, source_target_pairs={{0,32},{32,64},{64,96},{96,128},{128,160},{160,192},{192,224},{224... | collective-permute-start | bytes 405512 | tf_op jit(solution)/shard_map/ppermute | solution.py:14
  4.7 7.4 %collective-permute-start.1 = (f32[33,1,8,128]{3,1,2,0:T(1,128)S(1)}, f32[33,1,8,128]{3,1,2,0:T(1,128)S(1)}, u32[]{:S(2)}, u32[]{:S(2)}) collective-permute-start(f32[33,1,8,128]{3,1,2,0:T(1,128)S(1)} %get-tuple-element.21), channel_id=1, source_target_pairs={{32,0},{64,32},{96,64},{128,96},{160,128},{192,160},{224,192},{256... | collective-permute-start | bytes 405512 | tf_op jit(solution)/shard_map/ppermute | solution.py:15
  12.2 7.0 %collective-permute-start.2 = (f32[33,6,1,128]{3,1,2,0:T(8,128)S(1)}, f32[33,6,1,128]{3,1,2,0:T(8,128)S(1)}, u32[]{:S(2)}, u32[]{:S(2)}) collective-permute-start(f32[33,6,1,128]{3,1,2,0:T(8,128)S(1)} %get-tuple-element.16), channel_id=1, source_target_pairs={{0,4},{4,8},{8,12},{12,16},{16,20},{20,24},{24,28},{1,5},{5,9},{9,... | collective-permute-start | bytes 304136 | tf_op jit(solution)/shard_map/ppermute | solution.py:14
  16.5 7.5 %collective-permute-start.3 = (f32[33,6,1,128]{3,1,2,0:T(8,128)S(1)}, f32[33,6,1,128]{3,1,2,0:T(8,128)S(1)}, u32[]{:S(2)}, u32[]{:S(2)}) collective-permute-start(f32[33,6,1,128]{3,1,2,0:T(8,128)S(1)} %get-tuple-element.17), channel_id=1, source_target_pairs={{4,0},{8,4},{12,8},{16,12},{20,16},{24,20},{28,24},{5,1},{9,5},{13... | collective-permute-start | bytes 304136 | tf_op jit(solution)/shard_map/ppermute | solution.py:15
  19.2 4.8 copy-start.5
  23.9 0.7 copy-start.7
  26.0 7.0 %collective-permute-start.5 = (f32[33,6,10,1]{0,3,2,1:T(1,128)S(1)}, f32[33,6,10,1]{0,3,2,1:T(1,128)S(1)}, u32[]{:S(2)}, u32[]{:S(2)}) collective-permute-start(f32[33,6,10,1]{0,3,2,1:T(1,128)S(1)} %copy.33), channel_id=1, source_target_pairs={{1,0},{2,1},{3,2},{5,4},{6,5},{7,6},{9,8},{10,9},{11,10},{13,12},{... | collective-permute-start | bytes 23768 | tf_op jit(solution)/shard_map/ppermute | solution.py:15
  27.9 6.1 collective-permute-start.4
  35.5 1.0 copy-start.16
  35.5 1.1 copy-start.4
  35.5 1.1 copy-start.6
  35.5 1.1 copy-start.8
  36.6 5.3 copy-start.10
  36.6 5.3 copy-start.11
  36.6 5.3 copy-start.12
  36.6 5.3 copy-start.13
  36.6 5.3 copy-start.14
  36.6 5.3 copy-start.15
  41.9 22.5 %copy-start.1 = (f32[32,4,8,128]{3,1,2,0:T(4,128)}, f32[32,4,8,128]{3,1,2,0:T(4,128)S(1)}, u32[]{:S(2)}) copy-start(f32[32,4,8,128]{3,1,2,0:T(4,128)S(1)} %fusion.36) | copy-start | bytes 1572868
  42.1 7.5 %collective-permute-start.7 = (f32[32,1,8,128]{3,1,2,0:T(1,128)S(1)}, f32[32,1,8,128]{3,1,2,0:T(1,128)S(1)}, u32[]{:S(2)}, u32[]{:S(2)}) collective-permute-start(f32[32,1,8,128]{3,1,2,0:T(1,128)S(1)} %get-tuple-element.22), channel_id=1, source_target_pairs={{0,32},{32,64},{64,96},{96,128},{128,160},{160,192},{192,224},{224... | collective-permute-start | bytes 393224 | tf_op jit(solution)/shard_map/ppermute | solution.py:14
  44.0 7.4 %collective-permute-start.6 = (f32[32,1,8,128]{3,1,2,0:T(1,128)S(1)}, f32[32,1,8,128]{3,1,2,0:T(1,128)S(1)}, u32[]{:S(2)}, u32[]{:S(2)}) collective-permute-start(f32[32,1,8,128]{3,1,2,0:T(1,128)S(1)} %get-tuple-element.23), channel_id=1, source_target_pairs={{32,0},{64,32},{96,64},{128,96},{160,128},{192,160},{224,192},{256... | collective-permute-start | bytes 393224 | tf_op jit(solution)/shard_map/ppermute | solution.py:15
  51.5 6.9 %collective-permute-start.9 = (f32[32,6,1,128]{3,1,2,0:T(8,128)S(1)}, f32[32,6,1,128]{3,1,2,0:T(8,128)S(1)}, u32[]{:S(2)}, u32[]{:S(2)}) collective-permute-start(f32[32,6,1,128]{3,1,2,0:T(8,128)S(1)} %get-tuple-element.18), channel_id=1, source_target_pairs={{0,4},{4,8},{8,12},{12,16},{16,20},{20,24},{24,28},{1,5},{5,9},{9,... | collective-permute-start | bytes 294920 | tf_op jit(solution)/shard_map/ppermute | solution.py:14
  55.8 8.6 %collective-permute-start.8 = (f32[32,6,1,128]{3,1,2,0:T(8,128)S(1)}, f32[32,6,1,128]{3,1,2,0:T(8,128)S(1)}, u32[]{:S(2)}, u32[]{:S(2)}) collective-permute-start(f32[32,6,1,128]{3,1,2,0:T(8,128)S(1)} %get-tuple-element.19), channel_id=1, source_target_pairs={{4,0},{8,4},{12,8},{16,12},{20,16},{24,20},{28,24},{5,1},{9,5},{13... | collective-permute-start | bytes 294920 | tf_op jit(solution)/shard_map/ppermute | solution.py:15
  64.4 0.7 copy-start.9
  66.3 6.9 %collective-permute-start.10 = (f32[32,6,10,1]{0,3,2,1:T(1,128)S(1)}, f32[32,6,10,1]{0,3,2,1:T(1,128)S(1)}, u32[]{:S(2)}, u32[]{:S(2)}) collective-permute-start(f32[32,6,10,1]{0,3,2,1:T(1,128)S(1)} %copy.45), channel_id=1, source_target_pairs={{1,0},{2,1},{3,2},{5,4},{6,5},{7,6},{9,8},{10,9},{11,10},{13,12},{... | collective-permute-start | bytes 23048 | tf_op jit(solution)/shard_map/ppermute | solution.py:15
  68.2 6.8 collective-permute-start.11
  76.6 6.7 copy-start
  191.0 0.8 copy-start.3
  295.3 0.8 copy-start.2
